TPU v7x, 32 devices: a whole 2x2x4 slice. The times are simulated.
32 devices in a mesh: gx: 4 (over z), gy: 4 (over x, core), gz: 2 (over y).
Axes of the slice: x: 2, y: 2, z: 4, core: 2. Of those that a mesh axis runs over, the one named last changes fastest.
Arguments:
- phase: int32 [4, 8, 64], P('gx', 'gy', 'gz'), may hold values from 0 to 1
- lame: float32 [2, 2], replicated, may hold values from 0.3 to 10
- start: float32 [3, 32, 16, 32, 256], P(None, None, 'gx', 'gy', 'gz'), may hold values from -6 to 6
Outputs:
- basis: float32 [3, 32, 16, 32, 256], P(None, None, 'gx', 'gy', 'gz')
- coarse: float32 [32, 32], replicated
All inputs are finite; a program needn't handle non-finite values.
Results may differ from a plain program's by a relative error of at most 0.0001.
Values sent between devices are 32-bit elements; how exact they have to be, the bound alone decides.
A program may use at most 64 MiB of HBM per device.

v0:
```python
import functools

import jax
import jax.numpy as jnp
from jax import lax
from jax.experimental import pallas as pl
from jax.experimental.pallas import tpu as pltpu
from jax.sharding import PartitionSpec as P

ITERS = 3
PHASES = 2
BRICK = 4
PIECES = 3
UNROLL = 2
AXES = ("gx", "gy", "gz")
MESH = pl.DeviceIdType.MESH
F32 = jnp.float32
BF16 = jnp.bfloat16


def split(value):
    pieces = []
    for _ in range(PIECES):
        piece = value.astype(BF16)
        pieces.append(piece)
        value = value - piece.astype(F32)
    return jnp.concatenate(pieces, axis=0)


def contract_last(left, right):
    return lax.dot_general(
        left, right, (((1,), (1,)), ((), ())), preferred_element_type=F32
    )


def exact_dot(left, right):
    return jnp.dot(
        left, right, precision=lax.Precision.HIGHEST, preferred_element_type=F32
    )


def fold(blocks, size):
    rows = blocks[:size]
    for k in range(1, PIECES):
        rows = rows + blocks[k * size : (k + 1) * size]
    total = rows[:, :size]
    for k in range(1, PIECES):
        total = total + rows[:, k * size : (k + 1) * size]
    return total


def inverse_factor(gram, size):
    row = lax.broadcasted_iota(jnp.int32, (size, size), 0)
    col = lax.broadcasted_iota(jnp.int32, (size, size), 1)
    both = jnp.concatenate([gram, jnp.where(row == col, 1.0, 0.0).astype(F32)], axis=1)
    rows = lax.broadcasted_iota(jnp.int32, both.shape, 0)
    for j in range(size):
        scale = lax.rsqrt(both[j : j + 1, j : j + 1])
        pivot = both[j : j + 1, :] * scale
        column = both[:, j : j + 1] * scale
        both = jnp.where(
            rows > j, both - column * pivot, jnp.where(rows == j, pivot, both)
        )
    return both[:, size:]


def kernel(
    counts,
    dims,
    lame,
    phase,
    start,
    basis,
    coarse,
    field,
    stage,
    edge_out,
    edge_in,
    edge_now,
    phase_own,
    phase_in,
    weights,
    parts,
    image_parts,
    sums,
    local_sem,
    phase_send,
    phase_recv,
    send_sem,
    recv_sem,
    sum_send,
    sum_recv,
):
    parts_c, vecs, nx, ny, nz = dims
    nodes = nx * ny
    total_rows = 1.0 * parts_c * nodes * nz * counts[0] * counts[1] * counts[2]
    me = [lax.axis_index(axis) for axis in AXES]
    half = ny // 2

    loads = [
        pltpu.make_async_copy(start.at[c], stage.at[c], local_sem.at[c])
        for c in range(parts_c)
    ]
    for copy in loads:
        copy.start()

    def has(side):
        axis = side // 2
        return me[axis] > 0 if side % 2 == 0 else me[axis] < counts[axis] - 1

    def lacks(side):
        axis = side // 2
        return me[axis] == 0 if side % 2 == 0 else me[axis] == counts[axis] - 1

    def beside(side):
        axis = side // 2
        return {AXES[axis]: me[axis] - 1 if side % 2 == 0 else me[axis] + 1}

    plane = jnp.zeros((vecs, nz), F32)
    for side in range(2):
        at = 0 if side == 0 else nx + 1

        @pl.when(lacks(side))
        def _(at=at):
            def clear(i, _):
                for s in range(ITERS + 1):
                    for c in range(parts_c):
                        field[s, c, at, i + 1] = plane
                return 0

            lax.fori_loop(0, ny, clear, 0)

    for side in range(2, 4):
        at = 0 if side == 2 else ny + 1

        @pl.when(lacks(side))
        def _(at=at):
            def clear(i, _):
                for s in range(ITERS + 1):
                    for c in range(parts_c):
                        field[s, c, i + 1, at] = plane
                return 0

            lax.fori_loop(0, nx, clear, 0)

    def clear_half(i, _):
        for c in range(parts_c):
            field[ITERS, c, 0, half + i + 1] = plane
            field[ITERS, c, nx + 1, i + 1] = plane
        return 0

    lax.fori_loop(0, half, clear_half, 0)
    edge_in[...] = jnp.zeros(edge_in.shape, F32)
    phase_in[...] = jnp.zeros(phase_in.shape, F32)

    bricks_x, bricks_y, bricks_z = phase.shape
    spread = jnp.where(
        lax.broadcasted_iota(jnp.int32, (bricks_z, nz), 1) // BRICK
        == lax.broadcasted_iota(jnp.int32, (bricks_z, nz), 0),
        1.0,
        0.0,
    ).astype(F32)
    row_brick = lax.broadcasted_iota(jnp.int32, (ny, bricks_z), 0) // BRICK
    for bx in range(bricks_x):
        own = phase[bx].astype(F32)
        rows = jnp.zeros((ny, bricks_z), F32)
        for by in range(bricks_y):
            rows = jnp.where(
                row_brick == by,
                jnp.broadcast_to(own[by : by + 1], (ny, bricks_z)),
                rows,
            )
        phase_own[bx] = jnp.dot(rows, spread, preferred_element_type=F32)

    barrier = pltpu.get_barrier_semaphore()
    for axis in range(3):
        for k in range(counts[axis]):

            @pl.when(me[axis] != k)
            def _(axis=axis, k=k):
                pl.semaphore_signal(
                    barrier, inc=1, device_id={AXES[axis]: k}, device_id_type=MESH
                )

    def face(s, c, side):
        if side == 0:
            src, dst = field.at[s, c, 1], field.at[s, c, nx + 1]
        elif side == 1:
            src, dst = field.at[s, c, nx], field.at[s, c, 0]
        elif side == 2:
            src = field.at[s, c, pl.ds(1, nx), 1]
            dst = field.at[s, c, pl.ds(1, nx), ny + 1]
        elif side == 3:
            src = field.at[s, c, pl.ds(1, nx), ny]
            dst = field.at[s, c, pl.ds(1, nx), 0]
        else:
            src, dst = edge_out.at[s, c], edge_in.at[s, c, 1 - side % 2]
        if side < 2:
            if s < ITERS:
                rows = pl.ds(1, ny)
            elif side == 0:
                rows = pl.ds(half + 1, ny - half)
            else:
                rows = pl.ds(1, half)
            src, dst = src.at[rows], dst.at[rows]
        return src, dst

    def send_copy(s, c, side):
        src, dst = face(s, c, side)
        return pltpu.make_async_remote_copy(
            src_ref=src,
            dst_ref=dst,
            send_sem=send_sem.at[s, c, side],
            recv_sem=recv_sem.at[s, c, side ^ 1],
            device_id=beside(side),
            device_id_type=MESH,
        )

    def recv_copy(s, c, side):
        src, dst = face(s, c, side ^ 1)
        return pltpu.make_async_remote_copy(
            src_ref=src,
            dst_ref=dst,
            send_sem=send_sem.at[s, c, side],
            recv_sem=recv_sem.at[s, c, side],
            device_id=beside(side),
            device_id_type=MESH,
        )

    def each_side(action):
        for side in range(6):

            @pl.when(has(side))
            def _(side=side):
                action(side)

    def send(s, c):
        each_side(lambda side: send_copy(s, c, side).start())

    def receive(s, c):
        each_side(lambda side: recv_copy(s, c, side).wait_recv())

    def phase_copy(side, signal):
        return pltpu.make_async_remote_copy(
            src_ref=phase_own,
            dst_ref=phase_in.at[signal],
            send_sem=phase_send.at[side],
            recv_sem=phase_recv.at[signal],
            device_id=beside(side),
            device_id_type=MESH,
        )

    lane = lax.broadcasted_iota(jnp.int32, (vecs, nz), 1)
    empty = jnp.zeros((vecs, nz), F32)

    def take_edges(edges, value, i):
        here = lax.rem(lane + (nz + 1 - 2 * i), nz) < 2
        return jnp.where(here, pltpu.roll(value, 2 * i, 1), edges)

    for c in range(parts_c):
        loads[c].wait()

        def bring(k, edges, c=c):
            for t in range(UNROLL):
                i = k * UNROLL + t
                value = stage[c, pl.ds(i, vecs, stride=nodes), :]
                field[0, c, i // ny + 1, lax.rem(i, ny) + 1] = value
                edges = take_edges(edges, value, i)
            return edges

        edge_out[0, c] = lax.fori_loop(0, nodes // UNROLL, bring, empty)
        if c == 0:
            pl.semaphore_wait(barrier, sum(counts) - 3)
            each_side(lambda side: phase_copy(side, side ^ 1).start())
        send(0, c)

    each_side(lambda side: phase_copy(side, side).wait_recv())
    line = lax.broadcasted_iota(jnp.int32, (ny, nz), 0)
    across = lax.broadcasted_iota(jnp.int32, (ny, nz), 1)

    def material(kinds):
        shear = jnp.zeros(kinds.shape, F32)
        first = jnp.zeros(kinds.shape, F32)
        for index in range(PHASES):
            hit = kinds == float(index)
            shear = shear + jnp.where(hit, lame[index, 0], 0.0)
            first = first + jnp.where(hit, lame[index, 1], 0.0)
        return shear, first + shear

    for x in range(nx):
        bx = x // BRICK
        own = phase_own[bx]
        others = [
            phase_own[(x - 1) // BRICK] if x > 0 else phase_in[0, bricks_x - 1],
            phase_own[(x + 1) // BRICK] if x < nx - 1 else phase_in[1, 0],
            pltpu.roll(jnp.where(line == ny - 1, phase_in[2, bx], own), 1, 0),
            pltpu.roll(jnp.where(line == 0, phase_in[3, bx], own), ny - 1, 0),
            pltpu.roll(jnp.where(across == nz - 1, phase_in[4, bx], own), 1, 1),
            pltpu.roll(jnp.where(across == 0, phase_in[5, bx], own), nz - 1, 1),
        ]
        shear_c, grow_c = material(own)
        for side in range(6):
            shear_n, grow_n = material(others[side])
            w_shear = 0.5 * (shear_c + shear_n)
            w_grow = 0.5 * (grow_c + grow_n)
            weights[2 * side, pl.ds(x * ny, ny), :] = w_shear
            weights[2 * side + 1, pl.ds(x * ny, ny), :] = w_shear + w_grow

    def image(s, c, i):
        x, y = i // ny, lax.rem(i, ny)
        centre = field[s, c, x + 1, y + 1]
        border = pltpu.roll(edge_now[...], lax.rem(2 * nz - 2 * i, nz), 1)
        others = [
            field[s, c, x, y + 1],
            field[s, c, x + 2, y + 1],
            field[s, c, x + 1, y],
            field[s, c, x + 1, y + 2],
            pltpu.roll(jnp.where(lane == nz - 1, border, centre), 1, 1),
            pltpu.roll(jnp.where(lane == 0, border, centre), nz - 1, 1),
        ]
        total = None
        for side in range(6):
            which = 2 * side + (1 if side // 2 == c else 0)
            weight = weights[which, pl.ds(i, 1), :]
            term = weight * (centre - others[side])
            total = term if total is None else total + term
        return total

    def ready(s, c):
        receive(s, c)
        edge_now[...] = jnp.where(
            lax.rem(lane, 2) == 0, edge_in[s, c, 1], edge_in[s, c, 0]
        )

    def product(c, other):
        def body(x, total):
            left = jnp.concatenate(
                [parts[c, x * ny + y] for y in range(ny)], axis=1
            )
            right = (
                left
                if other is None
                else jnp.concatenate([other[x * ny + y] for y in range(ny)], axis=1)
            )
            return total + contract_last(left, right)

        size = PIECES * vecs
        return lax.fori_loop(0, nx, body, jnp.zeros((size, size), F32))

    offsets = [0, counts[0], counts[0] + counts[1]]

    def sum_copy(which, axis, slot, other):
        at = offsets[axis] + slot
        return pltpu.make_async_remote_copy(
            src_ref=sums.at[which, at],
            dst_ref=sums.at[which, at],
            send_sem=sum_send.at[which, offsets[axis] + other],
            recv_sem=sum_recv.at[which, at],
            device_id={AXES[axis]: other},
            device_id_type=MESH,
        )

    def sum_start(which, axis, value):
        sums[which, offsets[axis] + me[axis]] = value
        for k in range(counts[axis]):

            @pl.when(me[axis] != k)
            def _(k=k):
                sum_copy(which, axis, me[axis], k).start()

    def sum_end(which, axis):
        for k in range(counts[axis]):

            @pl.when(me[axis] != k)
            def _(k=k):
                sum_copy(which, axis, k, k).wait_recv()

        total = sums[which, offsets[axis]]
        for k in range(1, counts[axis]):
            total = total + sums[which, offsets[axis] + k]
        return total

    def padded(square):
        return jnp.concatenate([square, jnp.zeros((vecs, nz - vecs), F32)], axis=1)

    gram = None
    for s in range(ITERS):
        last = s == ITERS - 1
        for c in range(parts_c):
            ready(s, c)

            def step(k, edges, s=s, c=c, last=last):
                for t in range(UNROLL):
                    i = k * UNROLL + t
                    value = image(s, c, i)
                    field[s + 1, c, i // ny + 1, lax.rem(i, ny) + 1] = value
                    edges = take_edges(edges, value, i)
                    if last:
                        parts[c, i] = split(value)
                return edges

            edge_out[s + 1, c] = lax.fori_loop(0, nodes // UNROLL, step, empty)
            send(s + 1, c)
            if last:
                more = product(c, None)
                gram = more if gram is None else gram + more

    sum_start(0, 0, padded(fold(gram, vecs)))

    cross = None
    value = None
    for c in range(parts_c):
        ready(ITERS, c)

        def twice(y, _, c=c):
            low = field[ITERS, c, 0, y + 1]
            high = field[ITERS, c, nx + 1, half + y + 1]
            field[ITERS, c, 0, y + 1] = low + low
            field[ITERS, c, nx + 1, half + y + 1] = high + high
            return 0

        lax.fori_loop(0, half, twice, 0)

        def last_step(k, _, c=c):
            for t in range(UNROLL):
                i = k * UNROLL + t
                image_parts[i] = split(image(ITERS, c, i))
            return 0

        lax.fori_loop(0, nodes // UNROLL, last_step, 0)
        more = product(c, image_parts)
        cross = more if cross is None else cross + more
        value = sum_end(0, c)
        if c < 2:
            sum_start(0, c + 1, value)

    sum_start(1, 0, padded(fold(cross, vecs)))
    mixing = inverse_factor(value[:, :vecs] / total_rows, vecs)
    pieces = split(mixing)
    high, middle, low = (pieces[k * vecs : (k + 1) * vecs] for k in range(PIECES))
    none = jnp.zeros((vecs, vecs), BF16)
    mixer = jnp.concatenate(
        [
            jnp.concatenate([high, high, high], axis=1),
            jnp.concatenate([middle, middle, none], axis=1),
            jnp.concatenate([low, none, none], axis=1),
        ],
        axis=0,
    )

    stores = []
    for c in range(parts_c):

        def mix(k, _, c=c):
            for t in range(UNROLL):
                i = k * UNROLL + t
                out = jnp.dot(mixer, parts[c, i], preferred_element_type=F32)
                stage[c, pl.ds(i, vecs, stride=nodes), :] = (
                    out[:vecs] + out[vecs : 2 * vecs] + out[2 * vecs :]
                )
            return 0

        lax.fori_loop(0, nodes // UNROLL, mix, 0)
        copy = pltpu.make_async_copy(stage.at[c], basis.at[c], local_sem.at[c])
        copy.start()
        stores.append(copy)
        value = sum_end(1, c)
        if c < 2:
            sum_start(1, c + 1, value)

    form = value[:, :vecs]
    form = 0.5 * (form + form.T)
    first = exact_dot(mixing, form)
    coarse[...] = (
        lax.dot_general(
            first,
            mixing,
            (((1,), (1,)), ((), ())),
            precision=lax.Precision.HIGHEST,
            preferred_element_type=F32,
        )
        / total_rows
    )

    for s in range(ITERS + 1):
        for c in range(parts_c):
            each_side(lambda side: send_copy(s, c, side).wait_send())
    each_side(lambda side: phase_copy(side, side ^ 1).wait_send())
    for which in range(2):
        for axis in range(3):
            for k in range(counts[axis]):

                @pl.when(me[axis] != k)
                def _(which=which, axis=axis, k=k):
                    sum_copy(which, axis, me[axis], k).wait_send()

    for copy in stores:
        copy.wait()


def on_device(counts, phase, lame, start):
    comps, vecs, nx, ny, nz = dims = start.shape
    nodes = nx * ny
    assert comps == 3 and 2 * nodes <= nz and ny % 2 == 0
    slots = sum(counts)
    steps = ITERS + 1
    basis, coarse = pl.pallas_call(
        functools.partial(kernel, counts, dims),
        out_shape=(
            jax.ShapeDtypeStruct((comps, vecs * nodes, nz), F32),
            jax.ShapeDtypeStruct((vecs, vecs), F32),
        ),
        in_specs=[
            pl.BlockSpec(memory_space=pltpu.SMEM),
            pl.BlockSpec(memory_space=pltpu.VMEM),
            pl.BlockSpec(memory_space=pl.ANY),
        ],
        out_specs=(
            pl.BlockSpec(memory_space=pl.ANY),
            pl.BlockSpec(memory_space=pltpu.VMEM),
        ),
        scratch_shapes=[
            pltpu.VMEM((steps, comps, nx + 2, ny + 2, vecs, nz), F32),
            pltpu.VMEM((comps, vecs * nodes, nz), F32),
            pltpu.VMEM((steps, comps, vecs, nz), F32),
            pltpu.VMEM((steps, comps, 2, vecs, nz), F32),
            pltpu.VMEM((vecs, nz), F32),
            pltpu.VMEM((phase.shape[0], ny, nz), F32),
            pltpu.VMEM((6, phase.shape[0], ny, nz), F32),
            pltpu.VMEM((12, nodes, nz), F32),
            pltpu.VMEM((comps, nodes, PIECES * vecs, nz), BF16),
            pltpu.VMEM((nodes, PIECES * vecs, nz), BF16),
            pltpu.VMEM((2, slots, vecs, nz), F32),
            pltpu.SemaphoreType.DMA((comps,)),
            pltpu.SemaphoreType.DMA((6,)),
            pltpu.SemaphoreType.DMA((6,)),
            pltpu.SemaphoreType.DMA((steps, comps, 6)),
            pltpu.SemaphoreType.DMA((steps, comps, 6)),
            pltpu.SemaphoreType.DMA((2, slots)),
            pltpu.SemaphoreType.DMA((2, slots)),
        ],
        compiler_params=pltpu.CompilerParams(
            collective_id=0, has_side_effects=True, vmem_limit_bytes=48 * 1024 * 1024
        ),
    )(lame, phase, start.reshape(comps, vecs * nodes, nz))
    return basis.reshape(start.shape), coarse


def solution(mesh):
    counts = tuple(mesh.shape[axis] for axis in AXES)
    spread = P(None, None, *AXES)
    return jax.shard_map(
        functools.partial(on_device, counts),
        mesh=mesh,
        in_specs=(P(*AXES), P(), spread),
        out_specs=(spread, P()),
        check_vma=False,
    )
```

profile of v0, /device:TPU:0, one launch (start us, length us, event | category | flops | bytes accessed | tf_op | source)
XLA Modules:
  0.0 88.1 jit_solution(1800734426346380635)
XLA Ops:
  0.6 0.0 copy-start
  0.6 1.4 %copy-done = f32[3,32,4,8,128]{4,3,2,1,0:T(8,128)S(1)} copy-done((f32[3,32,4,8,128]{4,3,2,1,0:T(8,128)S(1)}, f32[3,32,4,8,128]{4,3,2,1,0:T(8,128)}, u32[]{:S(2)}) %copy-start) | copy-done | bytes 1572888
  2.0 0.0 copy-start.1
  2.0 0.7 copy-done.1
  2.7 0.0 copy-start.2
  2.7 0.7 copy-done.2
  3.4 83.0 %shard_map.50 = (f32[3,1024,128]{2,1,0:T(8,128)S(1)}, f32[32,32]{1,0:T(8,128)S(1)}) custom-call(f32[2,2]{1,0:T(2,128)S(1)} %copy-done.1, s32[1,2,32]{2,1,0:T(2,128)S(1)} %copy-done.2, f32[3,1024,128]{2,1,0:T(8,128)S(1)} %bitcast.2), custom_call_target="tpu_custom_call" | custom-call | tf_op jit(solution)/shard_map/pallas_call | solution.py:507
  86.4 1.1 %copy.7 = f32[3,32,4,8,128]{4,3,2,1,0:T(8,128)} copy(f32[3,32,4,8,128]{4,3,2,1,0:T(8,128)S(1)} %bitcast.3) | data formatting | bytes 3145728
  87.5 0.6 copy.8
Async XLA Ops:
  0.6 1.4 %copy-start = (f32[3,32,4,8,128]{4,3,2,1,0:T(8,128)S(1)}, f32[3,32,4,8,128]{4,3,2,1,0:T(8,128)}, u32[]{:S(2)}) copy-start(f32[3,32,4,8,128]{4,3,2,1,0:T(8,128)} %param.5) | copy-start | bytes 4718596
  2.0 0.7 copy-start.1
  2.7 0.7 copy-start.2
where the time goes:
time: 88.3 us; the launch traced here: 88.1 us
  Pallas kernels  83 us (94%)
  local copies, waits for them, and re-layouts  4.51 us (5%)
    pallas_call x1, Pallas kernels, on_device(): pl.pallas_call(functools.partial(kernel, counts, dims), out_shape=(jax.Sh...  83 us
    unnamed x8, local copies, waits for them, and re-layouts  4.51 us

commit v1 on v0

--- a/solution.py
+++ b/solution.py
@@ -11,7 +11,7 @@
 PHASES = 2
 BRICK = 4
 PIECES = 3
-UNROLL = 2
+GROUP = 4
 AXES = ("gx", "gy", "gz")
 MESH = pl.DeviceIdType.MESH
 F32 = jnp.float32
@@ -67,11 +67,13 @@
 def kernel(
     counts,
     dims,
-    lame,
-    phase,
+    lame_in,
+    phase_hbm,
     start,
     basis,
     coarse,
+    lame,
+    phase,
     field,
     stage,
     edge_out,
@@ -97,12 +99,32 @@
     me = [lax.axis_index(axis) for axis in AXES]
     half = ny // 2
 
-    loads = [
-        pltpu.make_async_copy(start.at[c], stage.at[c], local_sem.at[c])
-        for c in range(parts_c)
+    small = [
+        pltpu.make_async_copy(phase_hbm, phase, local_sem.at[parts_c]),
+        pltpu.make_async_copy(lame_in, lame, local_sem.at[parts_c + 1]),
     ]
-    for copy in loads:
+    for copy in small:
         copy.start()
+
+    def place(k):
+        each = ny // GROUP
+        return lax.div(k, each), lax.rem(k, each) * GROUP, k * GROUP
+
+    for c in range(parts_c):
+
+        def fetch(k, _, c=c):
+            x, y, _i = place(k)
+            for t in range(GROUP):
+                pltpu.make_async_copy(
+                    start.at[c, :, x, y + t],
+                    field.at[0, c, x + 1, y + t + 1],
+                    local_sem.at[c],
+                ).start()
+            return 0
+
+        lax.fori_loop(0, nodes // GROUP, fetch, 0)
+
+    inner = (pl.ds(1, nx), pl.ds(1, ny))
 
     def has(side):
         axis = side // 2
@@ -153,6 +175,8 @@
     edge_in[...] = jnp.zeros(edge_in.shape, F32)
     phase_in[...] = jnp.zeros(phase_in.shape, F32)
 
+    for copy in small:
+        copy.wait()
     bricks_x, bricks_y, bricks_z = phase.shape
     spread = jnp.where(
         lax.broadcasted_iota(jnp.int32, (bricks_z, nz), 1) // BRICK
@@ -227,15 +251,26 @@
             device_id_type=MESH,
         )
 
-    def each_side(action):
-        for side in range(6):
+    lane = lax.broadcasted_iota(jnp.int32, (vecs, nz), 1)
+    pair = lax.rem(lax.div(lane + 1, 2), nz // 2)
+
+    def each_side(action, sides=range(6)):
+        for side in sides:
 
             @pl.when(has(side))
             def _(side=side):
                 action(side)
 
     def send(s, c):
-        each_side(lambda side: send_copy(s, c, side).start())
+        each_side(lambda side: send_copy(s, c, side).start(), range(4))
+        edges = jnp.zeros((vecs, nz), F32)
+        for i in range(nodes):
+            value = field[s, c, i // ny + 1, i % ny + 1]
+            edges = jnp.where(
+                pair == i, pltpu.roll(value, 2 * i, 1) if i else value, edges
+            )
+        edge_out[s, c] = edges
+        each_side(lambda side: send_copy(s, c, side).start(), range(4, 6))
 
     def receive(s, c):
         each_side(lambda side: recv_copy(s, c, side).wait_recv())
@@ -250,25 +285,10 @@
             device_id_type=MESH,
         )
 
-    lane = lax.broadcasted_iota(jnp.int32, (vecs, nz), 1)
-    empty = jnp.zeros((vecs, nz), F32)
-
-    def take_edges(edges, value, i):
-        here = lax.rem(lane + (nz + 1 - 2 * i), nz) < 2
-        return jnp.where(here, pltpu.roll(value, 2 * i, 1), edges)
-
     for c in range(parts_c):
-        loads[c].wait()
-
-        def bring(k, edges, c=c):
-            for t in range(UNROLL):
-                i = k * UNROLL + t
-                value = stage[c, pl.ds(i, vecs, stride=nodes), :]
-                field[0, c, i // ny + 1, lax.rem(i, ny) + 1] = value
-                edges = take_edges(edges, value, i)
-            return edges
-
-        edge_out[0, c] = lax.fori_loop(0, nodes // UNROLL, bring, empty)
+        pltpu.make_async_copy(
+            field.at[(1, c) + inner], field.at[(0, c) + inner], local_sem.at[c]
+        ).wait()
         if c == 0:
             pl.semaphore_wait(barrier, sum(counts) - 3)
             each_side(lambda side: phase_copy(side, side ^ 1).start())
@@ -306,34 +326,42 @@
             weights[2 * side, pl.ds(x * ny, ny), :] = w_shear
             weights[2 * side + 1, pl.ds(x * ny, ny), :] = w_shear + w_grow
 
-    def image(s, c, i):
-        x, y = i // ny, lax.rem(i, ny)
-        centre = field[s, c, x + 1, y + 1]
-        border = pltpu.roll(edge_now[...], lax.rem(2 * nz - 2 * i, nz), 1)
-        others = [
-            field[s, c, x, y + 1],
-            field[s, c, x + 2, y + 1],
-            field[s, c, x + 1, y],
-            field[s, c, x + 1, y + 2],
-            pltpu.roll(jnp.where(lane == nz - 1, border, centre), 1, 1),
-            pltpu.roll(jnp.where(lane == 0, border, centre), nz - 1, 1),
-        ]
-        total = None
-        for side in range(6):
-            which = 2 * side + (1 if side // 2 == c else 0)
-            weight = weights[which, pl.ds(i, 1), :]
-            term = weight * (centre - others[side])
-            total = term if total is None else total + term
-        return total
+    def image(s, c, k):
+        x, y, i = place(k)
+        column = [field[s, c, x + 1, y + t] for t in range(GROUP + 2)]
+        edges = edge_now[...]
+        totals = []
+        for t in range(GROUP):
+            centre = column[t + 1]
+            border = pltpu.roll(edges, nz - 2 * t - 2 * i, 1)
+            others = [
+                field[s, c, x, y + t + 1],
+                field[s, c, x + 2, y + t + 1],
+                column[t],
+                column[t + 2],
+                jnp.where(lane == 0, border, pltpu.roll(centre, 1, 1)),
+                jnp.where(lane == nz - 1, border, pltpu.roll(centre, nz - 1, 1)),
+            ]
+            total = None
+            for side in range(6):
+                which = 2 * side + (1 if side // 2 == c else 0)
+                weight = weights[which, pl.ds(i + t, 1), :]
+                term = weight * (centre - others[side])
+                total = term if total is None else total + term
+            totals.append(total)
+        return totals
 
     def ready(s, c):
         receive(s, c)
         edge_now[...] = jnp.where(
-            lax.rem(lane, 2) == 0, edge_in[s, c, 1], edge_in[s, c, 0]
+            lax.rem(lane, 2) == 0,
+            pltpu.roll(edge_in[s, c, 0], 1, 1),
+            pltpu.roll(edge_in[s, c, 1], nz - 1, 1),
         )
 
     def product(c, other):
-        def body(x, total):
+        total = None
+        for x in range(nx):
             left = jnp.concatenate(
                 [parts[c, x * ny + y] for y in range(ny)], axis=1
             )
@@ -342,10 +370,9 @@
                 if other is None
                 else jnp.concatenate([other[x * ny + y] for y in range(ny)], axis=1)
             )
-            return total + contract_last(left, right)
-
-        size = PIECES * vecs
-        return lax.fori_loop(0, nx, body, jnp.zeros((size, size), F32))
+            more = contract_last(left, right)
+            total = more if total is None else total + more
+        return total
 
     offsets = [0, counts[0], counts[0] + counts[1]]
 
@@ -389,17 +416,17 @@
         for c in range(parts_c):
             ready(s, c)
 
-            def step(k, edges, s=s, c=c, last=last):
-                for t in range(UNROLL):
-                    i = k * UNROLL + t
-                    value = image(s, c, i)
-                    field[s + 1, c, i // ny + 1, lax.rem(i, ny) + 1] = value
-                    edges = take_edges(edges, value, i)
-                    if last:
-                        parts[c, i] = split(value)
-                return edges
-
-            edge_out[s + 1, c] = lax.fori_loop(0, nodes // UNROLL, step, empty)
+            def step(k, _, s=s, c=c, last=last):
+                x, y, i = place(k)
+                totals = image(s, c, k)
+                for t in range(GROUP):
+                    field[s + 1, c, x + 1, y + t + 1] = totals[t]
+                if last:
+                    for t in range(GROUP):
+                        parts[c, i + t] = split(totals[t])
+                return 0
+
+            lax.fori_loop(0, nodes // GROUP, step, 0)
             send(s + 1, c)
             if last:
                 more = product(c, None)
@@ -422,12 +449,12 @@
         lax.fori_loop(0, half, twice, 0)
 
         def last_step(k, _, c=c):
-            for t in range(UNROLL):
-                i = k * UNROLL + t
-                image_parts[i] = split(image(ITERS, c, i))
+            totals = image(ITERS, c, k)
+            for t in range(GROUP):
+                image_parts[k * GROUP + t] = split(totals[t])
             return 0
 
-        lax.fori_loop(0, nodes // UNROLL, last_step, 0)
+        lax.fori_loop(0, nodes // GROUP, last_step, 0)
         more = product(c, image_parts)
         cross = more if cross is None else cross + more
         value = sum_end(0, c)
@@ -448,22 +475,28 @@
         axis=0,
     )
 
-    stores = []
     for c in range(parts_c):
 
         def mix(k, _, c=c):
-            for t in range(UNROLL):
-                i = k * UNROLL + t
-                out = jnp.dot(mixer, parts[c, i], preferred_element_type=F32)
-                stage[c, pl.ds(i, vecs, stride=nodes), :] = (
-                    out[:vecs] + out[vecs : 2 * vecs] + out[2 * vecs :]
-                )
+            x, y, i = place(k)
+            right = jnp.concatenate([parts[c, i + t] for t in range(GROUP)], axis=1)
+            out = jnp.dot(mixer, right, preferred_element_type=F32)
+            out = out[:vecs] + out[vecs : 2 * vecs] + out[2 * vecs :]
+            for t in range(GROUP):
+                stage[c, x, y + t] = out[:, t * nz : (t + 1) * nz]
             return 0
 
-        lax.fori_loop(0, nodes // UNROLL, mix, 0)
-        copy = pltpu.make_async_copy(stage.at[c], basis.at[c], local_sem.at[c])
-        copy.start()
-        stores.append(copy)
+        lax.fori_loop(0, nodes // GROUP, mix, 0)
+
+        def put(k, _, c=c):
+            x, y, _i = place(k)
+            for t in range(GROUP):
+                pltpu.make_async_copy(
+                    stage.at[c, x, y + t], basis.at[c, :, x, y + t], local_sem.at[c]
+                ).start()
+            return 0
+
+        lax.fori_loop(0, nodes // GROUP, put, 0)
         value = sum_end(1, c)
         if c < 2:
             sum_start(1, c + 1, value)
@@ -494,34 +527,38 @@
                 def _(which=which, axis=axis, k=k):
                     sum_copy(which, axis, me[axis], k).wait_send()
 
-    for copy in stores:
-        copy.wait()
+    for c in range(parts_c):
+        pltpu.make_async_copy(
+            stage.at[c], field.at[(0, c) + inner], local_sem.at[c]
+        ).wait()
 
 
 def on_device(counts, phase, lame, start):
     comps, vecs, nx, ny, nz = dims = start.shape
     nodes = nx * ny
-    assert comps == 3 and 2 * nodes <= nz and ny % 2 == 0
+    assert comps == 3 and 2 * nodes <= nz and ny % GROUP == 0
     slots = sum(counts)
     steps = ITERS + 1
     basis, coarse = pl.pallas_call(
         functools.partial(kernel, counts, dims),
         out_shape=(
-            jax.ShapeDtypeStruct((comps, vecs * nodes, nz), F32),
+            jax.ShapeDtypeStruct(start.shape, F32),
             jax.ShapeDtypeStruct((vecs, vecs), F32),
         ),
         in_specs=[
-            pl.BlockSpec(memory_space=pltpu.SMEM),
-            pl.BlockSpec(memory_space=pltpu.VMEM),
-            pl.BlockSpec(memory_space=pl.ANY),
+            pl.BlockSpec(memory_space=pltpu.HBM),
+            pl.BlockSpec(memory_space=pltpu.HBM),
+            pl.BlockSpec(memory_space=pltpu.HBM),
         ],
         out_specs=(
-            pl.BlockSpec(memory_space=pl.ANY),
+            pl.BlockSpec(memory_space=pltpu.HBM),
             pl.BlockSpec(memory_space=pltpu.VMEM),
         ),
         scratch_shapes=[
+            pltpu.SMEM(lame.shape, F32),
+            pltpu.VMEM(phase.shape, jnp.int32),
             pltpu.VMEM((steps, comps, nx + 2, ny + 2, vecs, nz), F32),
-            pltpu.VMEM((comps, vecs * nodes, nz), F32),
+            pltpu.VMEM((comps, nx, ny, vecs, nz), F32),
             pltpu.VMEM((steps, comps, vecs, nz), F32),
             pltpu.VMEM((steps, comps, 2, vecs, nz), F32),
             pltpu.VMEM((vecs, nz), F32),
@@ -531,7 +568,7 @@
             pltpu.VMEM((comps, nodes, PIECES * vecs, nz), BF16),
             pltpu.VMEM((nodes, PIECES * vecs, nz), BF16),
             pltpu.VMEM((2, slots, vecs, nz), F32),
-            pltpu.SemaphoreType.DMA((comps,)),
+            pltpu.SemaphoreType.DMA((comps + 2,)),
             pltpu.SemaphoreType.DMA((6,)),
             pltpu.SemaphoreType.DMA((6,)),
             pltpu.SemaphoreType.DMA((steps, comps, 6)),
@@ -540,10 +577,10 @@
             pltpu.SemaphoreType.DMA((2, slots)),
         ],
         compiler_params=pltpu.CompilerParams(
-            collective_id=0, has_side_effects=True, vmem_limit_bytes=48 * 1024 * 1024
+            collective_id=0, has_side_effects=True, vmem_limit_bytes=67043328
         ),
-    )(lame, phase, start.reshape(comps, vecs * nodes, nz))
-    return basis.reshape(start.shape), coarse
+    )(lame, phase, start)
+    return basis, coarse
 
 
 def solution(mesh):

time: 88.3 us -> 64.1 us (0.73)
  Pallas kernels: 83 us -> 59.9 us
  local copies, waits for them, and re-layouts: 4.51 us -> 3.28 us
    pallas_call x1, Pallas kernels: 83 us -> 59.9 us  [on_device(): pl.pallas_call(functools.partial(kernel, counts, dims), out_shape=(jax.Sh...]
    unnamed x8 -> x4, local copies, waits for them, and re-layouts: 4.51 us -> 3.28 us
where the time goes in v1:
time: 64.1 us; the launch traced here: 63.8 us
  Pallas kernels  59.9 us (93%)
  local copies, waits for them, and re-layouts  3.28 us (5%)
  between operations  0.65 us (1%)
    pallas_call x1, Pallas kernels, on_device(): pl.pallas_call(functools.partial(kernel, counts, dims), out_shape=(jax.Sh...  59.9 us
    unnamed x4, local copies, waits for them, and re-layouts  3.28 us

profile of v1, /device:TPU:0, one launch (start us, length us, event | category | flops | bytes accessed | tf_op | source)
XLA Modules:
  0.0 63.8 jit_solution(15651688125207748953)
XLA Ops:
  0.6 59.9 %shard_map.50 = (f32[3,32,4,8,128]{4,3,2,1,0:T(8,128)}, f32[32,32]{1,0:T(8,128)}) custom-call(f32[2,2]{1,0:T(2,128)} %lame_in.1, s32[1,2,32]{2,1,0:T(2,128)} %phase_hbm.1, f32[3,32,4,8,128]{4,3,2,1,0:T(8,128)} %start.1), custom_call_target="tpu_custom_call" | custom-call | tf_op jit(solution)/shard_map/pallas_call | solution.py:542
  60.5 0.0 copy-start
  60.6 2.7 %copy.7 = f32[3,32,4,8,128]{4,3,2,1,0:T(8,128)} copy(f32[3,32,4,8,128]{4,3,2,1,0:T(8,128)} %get-tuple-element.4) | data formatting | bytes 3145728
  63.2 0.0 copy-done
  63.2 0.6 copy.8
Async XLA Ops:
  60.5 2.7 %copy-start = (f32[32,32]{1,0:T(8,128)S(1)}, f32[32,32]{1,0:T(8,128)}, u32[]{:S(2)}) copy-start(f32[32,32]{1,0:T(8,128)} %get-tuple-element.5) | copy-start | bytes 12292

commit v2 on v1

--- a/solution.py
+++ b/solution.py
@@ -175,6 +175,22 @@
     edge_in[...] = jnp.zeros(edge_in.shape, F32)
     phase_in[...] = jnp.zeros(phase_in.shape, F32)
 
+    groups = (
+        [{"gy": y, "gz": z} for y in range(counts[1]) for z in range(counts[2])],
+        [{"gx": x} for x in range(counts[0])],
+    )
+    places = (me[1] * counts[2] + me[2], me[0])
+    offsets = (0, len(groups[0]))
+    barrier = pltpu.get_barrier_semaphore()
+    for own_at, members in zip(places, groups):
+        for k, member in enumerate(members):
+
+            @pl.when(own_at != k)
+            def _(member=member):
+                pl.semaphore_signal(
+                    barrier, inc=1, device_id=member, device_id_type=MESH
+                )
+
     for copy in small:
         copy.wait()
     bricks_x, bricks_y, bricks_z = phase.shape
@@ -195,16 +211,6 @@
                 rows,
             )
         phase_own[bx] = jnp.dot(rows, spread, preferred_element_type=F32)
-
-    barrier = pltpu.get_barrier_semaphore()
-    for axis in range(3):
-        for k in range(counts[axis]):
-
-            @pl.when(me[axis] != k)
-            def _(axis=axis, k=k):
-                pl.semaphore_signal(
-                    barrier, inc=1, device_id={AXES[axis]: k}, device_id_type=MESH
-                )
 
     def face(s, c, side):
         if side == 0:
@@ -290,7 +296,7 @@
             field.at[(1, c) + inner], field.at[(0, c) + inner], local_sem.at[c]
         ).wait()
         if c == 0:
-            pl.semaphore_wait(barrier, sum(counts) - 3)
+            pl.semaphore_wait(barrier, len(groups[0]) + len(groups[1]) - 2)
             each_side(lambda side: phase_copy(side, side ^ 1).start())
         send(0, c)
 
@@ -374,41 +380,46 @@
             total = more if total is None else total + more
         return total
 
-    offsets = [0, counts[0], counts[0] + counts[1]]
-
-    def sum_copy(which, axis, slot, other):
-        at = offsets[axis] + slot
+    def sum_copy(which, stage_at, slot, other):
+        at = offsets[stage_at] + slot
         return pltpu.make_async_remote_copy(
             src_ref=sums.at[which, at],
             dst_ref=sums.at[which, at],
-            send_sem=sum_send.at[which, offsets[axis] + other],
+            send_sem=sum_send.at[which, offsets[stage_at] + other],
             recv_sem=sum_recv.at[which, at],
-            device_id={AXES[axis]: other},
+            device_id=groups[stage_at][other],
             device_id_type=MESH,
         )
 
-    def sum_start(which, axis, value):
-        sums[which, offsets[axis] + me[axis]] = value
-        for k in range(counts[axis]):
-
-            @pl.when(me[axis] != k)
+    def each_member(stage_at, action):
+        for k in range(len(groups[stage_at])):
+
+            @pl.when(places[stage_at] != k)
             def _(k=k):
-                sum_copy(which, axis, me[axis], k).start()
-
-    def sum_end(which, axis):
-        for k in range(counts[axis]):
-
-            @pl.when(me[axis] != k)
-            def _(k=k):
-                sum_copy(which, axis, k, k).wait_recv()
-
-        total = sums[which, offsets[axis]]
-        for k in range(1, counts[axis]):
-            total = total + sums[which, offsets[axis] + k]
+                action(k)
+
+    def sum_start(which, stage_at, value):
+        mine = places[stage_at]
+        sums[which, offsets[stage_at] + mine] = value
+        each_member(stage_at, lambda k: sum_copy(which, stage_at, mine, k).start())
+
+    def sum_end(which, stage_at):
+        each_member(stage_at, lambda k: sum_copy(which, stage_at, k, k).wait_recv())
+        total = sums[which, offsets[stage_at]]
+        for k in range(1, len(groups[stage_at])):
+            total = total + sums[which, offsets[stage_at] + k]
         return total
 
-    def padded(square):
-        return jnp.concatenate([square, jnp.zeros((vecs, nz - vecs), F32)], axis=1)
+    across_n = nz // vecs
+    down_n = vecs // across_n
+
+    def packed(square):
+        pieces = [square[k * down_n : (k + 1) * down_n] for k in range(across_n)]
+        return jnp.concatenate(pieces, axis=1)
+
+    def unpacked(value):
+        pieces = [value[:, k * vecs : (k + 1) * vecs] for k in range(across_n)]
+        return jnp.concatenate(pieces, axis=0)
 
     gram = None
     for s in range(ITERS):
@@ -432,10 +443,9 @@
                 more = product(c, None)
                 gram = more if gram is None else gram + more
 
-    sum_start(0, 0, padded(fold(gram, vecs)))
+    sum_start(0, 0, packed(fold(gram, vecs)))
 
     cross = None
-    value = None
     for c in range(parts_c):
         ready(ITERS, c)
 
@@ -457,12 +467,12 @@
         lax.fori_loop(0, nodes // GROUP, last_step, 0)
         more = product(c, image_parts)
         cross = more if cross is None else cross + more
-        value = sum_end(0, c)
-        if c < 2:
-            sum_start(0, c + 1, value)
-
-    sum_start(1, 0, padded(fold(cross, vecs)))
-    mixing = inverse_factor(value[:, :vecs] / total_rows, vecs)
+        if c == 0:
+            sum_start(0, 1, sum_end(0, 0))
+
+    sum_start(1, 0, packed(fold(cross, vecs)))
+    mixing = inverse_factor(unpacked(sum_end(0, 1)) / total_rows, vecs)
+    sum_start(1, 1, sum_end(1, 0))
     pieces = split(mixing)
     high, middle, low = (pieces[k * vecs : (k + 1) * vecs] for k in range(PIECES))
     none = jnp.zeros((vecs, vecs), BF16)
@@ -497,11 +507,7 @@
             return 0
 
         lax.fori_loop(0, nodes // GROUP, put, 0)
-        value = sum_end(1, c)
-        if c < 2:
-            sum_start(1, c + 1, value)
-
-    form = value[:, :vecs]
+    form = unpacked(sum_end(1, 1))
     form = 0.5 * (form + form.T)
     first = exact_dot(mixing, form)
     coarse[...] = (
@@ -520,12 +526,11 @@
             each_side(lambda side: send_copy(s, c, side).wait_send())
     each_side(lambda side: phase_copy(side, side ^ 1).wait_send())
     for which in range(2):
-        for axis in range(3):
-            for k in range(counts[axis]):
-
-                @pl.when(me[axis] != k)
-                def _(which=which, axis=axis, k=k):
-                    sum_copy(which, axis, me[axis], k).wait_send()
+        for stage_at in range(2):
+            each_member(
+                stage_at,
+                lambda k: sum_copy(which, stage_at, places[stage_at], k).wait_send(),
+            )
 
     for c in range(parts_c):
         pltpu.make_async_copy(
@@ -536,8 +541,9 @@
 def on_device(counts, phase, lame, start):
     comps, vecs, nx, ny, nz = dims = start.shape
     nodes = nx * ny
+    assert nz % vecs == 0 and vecs % (nz // vecs) == 0
     assert comps == 3 and 2 * nodes <= nz and ny % GROUP == 0
-    slots = sum(counts)
+    slots = counts[0] + counts[1] * counts[2]
     steps = ITERS + 1
     basis, coarse = pl.pallas_call(
         functools.partial(kernel, counts, dims),
@@ -567,7 +573,7 @@
             pltpu.VMEM((12, nodes, nz), F32),
             pltpu.VMEM((comps, nodes, PIECES * vecs, nz), BF16),
             pltpu.VMEM((nodes, PIECES * vecs, nz), BF16),
-            pltpu.VMEM((2, slots, vecs, nz), F32),
+            pltpu.VMEM((2, slots, vecs * vecs // nz, nz), F32),
             pltpu.SemaphoreType.DMA((comps + 2,)),
             pltpu.SemaphoreType.DMA((6,)),
             pltpu.SemaphoreType.DMA((6,)),

time: 64.1 us -> 57.4 us (0.90)
  Pallas kernels: 59.9 us -> 53.3 us
    pallas_call x1, Pallas kernels: 59.9 us -> 53.3 us  [on_device(): pl.pallas_call(functools.partial(kernel, counts, dims), out_shape=(jax.Sh...]
where the time goes in v2:
time: 57.4 us; the launch traced here: 57.2 us
  Pallas kernels  53.3 us (93%)
  local copies, waits for them, and re-layouts  3.28 us (6%)
  between operations  0.65 us (1%)
    pallas_call x1, Pallas kernels, on_device(): pl.pallas_call(functools.partial(kernel, counts, dims), out_shape=(jax.Sh...  53.3 us
    unnamed x4, local copies, waits for them, and re-layouts  3.28 us

profile of v2, /device:TPU:0, one launch (start us, length us, event | category | flops | bytes accessed | tf_op | source)
XLA Modules:
  0.0 57.2 jit_solution(7309841165597908582)
XLA Ops:
  0.6 53.3 %shard_map.50 = (f32[3,32,4,8,128]{4,3,2,1,0:T(8,128)}, f32[32,32]{1,0:T(8,128)}) custom-call(f32[2,2]{1,0:T(2,128)} %lame_in.1, s32[1,2,32]{2,1,0:T(2,128)} %phase_hbm.1, f32[3,32,4,8,128]{4,3,2,1,0:T(8,128)} %start.1), custom_call_target="tpu_custom_call" | custom-call | tf_op jit(solution)/shard_map/pallas_call | solution.py:548
  53.9 0.0 copy-start
  53.9 2.7 %copy.7 = f32[3,32,4,8,128]{4,3,2,1,0:T(8,128)} copy(f32[3,32,4,8,128]{4,3,2,1,0:T(8,128)} %get-tuple-element.4) | data formatting | bytes 3145728
  56.6 0.0 copy-done
  56.6 0.6 %copy.8 = f32[32,32]{1,0:T(8,128)} copy(f32[32,32]{1,0:T(8,128)S(1)} %copy-done) | data formatting | bytes 8192
Async XLA Ops:
  53.9 2.7 %copy-start = (f32[32,32]{1,0:T(8,128)S(1)}, f32[32,32]{1,0:T(8,128)}, u32[]{:S(2)}) copy-start(f32[32,32]{1,0:T(8,128)} %get-tuple-element.5) | copy-start | bytes 12292
